TPU v7x, 32 devices: a whole 2x2x4 slice. The times are simulated.
32 devices in a mesh: grp: 2 (over y), dev: 16 (over z, x, core).
Axes of the slice: x: 2, y: 2, z: 4, core: 2. Of those that a mesh axis runs over, the one named last changes fastest.
Arguments:
- spectra: bfloat16 [512, 2, 2048], P(('grp', 'dev')), may hold values from -6 to 6
- stack_in: bfloat16 [2, 256, 512, 128], P(None, None, ('grp', 'dev')), may hold values from -6 to 6
- plan: int32 [2], replicated, may hold values from 0 to 1
- seg_lengths: int32 [16], replicated, may hold values from 1 to 64, 512 in all
- taps: float32 [9], replicated, may hold values from -3 to 3
Outputs:
- stack: float32 [2, 256, 512, 128], P(None, None, ('grp', 'dev'))
- filtered: float32 [2, 256, 512, 128], P(None, None, ('grp', 'dev'))
All inputs are finite; a program needn't handle non-finite values.
Results may differ from a plain program's by a relative error of at most 0.0026.
Values may be sent and summed in bfloat16 or wider, within the bound.
No kernel may reach another device: no remote copies, remote signals or barrier semaphores. Data moves between devices by JAX's collectives and lax.ppermute only.
A program may use at most 64 MiB of HBM per device.

v0:
```python
import math
import jax
import jax.numpy as jnp
from jax import lax
from jax.sharding import PartitionSpec as P


def from_root(value, axis, source):
    kept = jnp.where(lax.axis_index(axis) == source, value, 0).astype(value.dtype)
    return lax.psum(kept, axis)


def extended_2(block, sides, width):
    for axis, dim in sides:
        count = lax.axis_size(axis)
        forward = [(i, i + 1) for i in range(count - 1)]
        backward = [(target, source) for source, target in forward]
        low = lax.ppermute(
            lax.slice_in_dim(block, block.shape[dim] - width, None, axis=dim), axis, forward
        )
        high = lax.ppermute(lax.slice_in_dim(block, 0, width, axis=dim), axis, backward)
        block = jnp.concatenate([low, block, high], axis=dim)
    return block


def whiten(spectra):
    real_part = spectra[:, 0, :].astype(jnp.float32)
    imag_part = spectra[:, 1, :].astype(jnp.float32)
    magnitude = jnp.sqrt(real_part * real_part + imag_part * imag_part)
    factor = 1.0 / jnp.maximum(magnitude, 0.25)
    return jnp.stack([real_part * factor, imag_part * factor], axis=1).astype(jnp.bfloat16)


def make_table(freqs, lags):
    bins = jnp.arange(freqs, dtype=jnp.int32)[:, None]
    shifts = jnp.arange(lags, dtype=jnp.int32)[None, :] - lags // 2
    modulus = bins * shifts % (2 * freqs)
    angle = modulus.astype(jnp.float32) * (math.pi / freqs)
    scale_value = 1.0 / math.sqrt(freqs)
    table = jnp.concatenate([jnp.cos(angle), -jnp.sin(angle)], axis=0) * scale_value
    return table.astype(jnp.bfloat16)


def cross_block(sources, receivers, table):
    src_re = sources[:, 0, :].astype(jnp.float32)[:, None, :]
    src_im = sources[:, 1, :].astype(jnp.float32)[:, None, :]
    rec_re = receivers[:, 0, :].astype(jnp.float32)[None, :, :]
    rec_im = receivers[:, 1, :].astype(jnp.float32)[None, :, :]
    cross_re = src_re * rec_re + src_im * rec_im
    cross_im = src_im * rec_re - src_re * rec_im
    cross = jnp.concatenate([cross_re, cross_im], axis=-1).astype(jnp.bfloat16)
    rows = sources.shape[0] * receivers.shape[0]
    flat = cross.reshape(rows, cross.shape[-1])
    result = jnp.dot(flat, table, preferred_element_type=jnp.float32)
    return result.reshape(sources.shape[0], receivers.shape[0], table.shape[1])


def segment_of(channel_ids, seg_lengths):
    bounds = jnp.cumsum(seg_lengths)[:-1]
    return jnp.sum((channel_ids[:, None] >= bounds[None, :]).astype(jnp.int32), axis=1)


def mixing_weights(seg_ids, taps, count):
    width = (taps.shape[0] - 1) // 2
    centre = seg_ids[width : width + count]
    columns = []
    for offset in range(taps.shape[0]):
        same = (seg_ids[offset : offset + count] == centre).astype(jnp.float32)
        columns.append(taps[offset] * same)
    return jnp.stack(columns, axis=1)


def apply_filter(extended, mixing, dim, count):
    total = jnp.zeros(extended.shape[:dim] + (count,) + extended.shape[dim + 1 :], jnp.float32)
    for offset in range(mixing.shape[1]):
        part = lax.slice_in_dim(extended, offset, offset + count, axis=dim)
        shape = [1] * extended.ndim
        shape[dim] = count
        total = total + mixing[:, offset].reshape(shape) * part
    return total


def shards(spectra, stack_in, plan, seg_lengths, taps):
    shard = spectra.shape[0]
    freqs = spectra.shape[2]
    steps = stack_in.shape[0]
    source_count = stack_in.shape[1]
    lags = stack_in.shape[3]
    width = (taps.shape[0] - 1) // 2
    group_channels = lax.axis_size("dev") * shard
    own = whiten(spectra)
    table = make_table(freqs, lags)
    block_rows = min(source_count, max(1, 512 // shard))
    start_channel = lax.axis_index(("grp", "dev")) * shard
    channel_ids = start_channel + jnp.arange(shard + 2 * width, dtype=jnp.int32) - width
    seg_ids = segment_of(channel_ids, seg_lengths)
    mixing = mixing_weights(seg_ids, taps, shard)
    stacks = []
    filtered_list = []
    for step in range(steps):
        first = plan[step] * source_count
        owner = first // group_channels
        offset = first % group_channels
        whole = lax.all_gather(own, "dev", axis=0, tiled=True)
        piece = lax.dynamic_slice_in_dim(whole, offset, source_count, 0)
        sources = from_root(piece, "grp", owner)
        grouped = sources.reshape(source_count // block_rows, block_rows, 2, freqs)
        corr = lax.map(lambda block: cross_block(block, own, table), grouped)
        corr = corr.reshape(source_count, shard, lags)
        updated = stack_in[step].astype(jnp.float32) + corr
        stacks.append(updated)
        extended = extended_2(updated, ((("grp", "dev"), 1),), width)
        filtered_list.append(apply_filter(extended, mixing, 1, shard))
    stack = jnp.stack(stacks, axis=0)
    filtered = jnp.stack(filtered_list, axis=0)
    return (stack, filtered)


def solution(mesh):
    placed = (P(("grp", "dev"), None, None), P(None, None, ("grp", "dev"), None), P(), P(), P())
    return jax.shard_map(
        shards,
        mesh=mesh,
        in_specs=placed,
        out_specs=(P(None, None, ("grp", "dev"), None), P(None, None, ("grp", "dev"), None)),
        check_vma=False,
    )
```

profile of v0, /device:TPU:1, one launch (start us, length us, event | category | flops | bytes accessed | tf_op | source)
XLA Modules:
  0.0 273.0 jit_solution(8880762887707342477)
XLA Ops:
  9.3 1.3 fusion.94
  12.0 42.2 %all-gather.2.cloned.1.call-done = bf16[256,2,2048]{2,0,1:T(8,128)(2,1)} async-done(((bf16[16,2,2048]{2,0,1:T(8,128)(2,1)}), bf16[256,2,2048]{2,0,1:T(8,128)(2,1)}) %all-gather.2.cloned.1.call-update) | async-done | bytes 2097168 | tf_op jit(solution)/shard_map/all_gather | solution.py:104
  54.1 1.9 broadcast_select_fusion.1
  56.0 1.5 copy.19
  57.4 1.5 copy.20
  60.6 1.3 compare_select_fusion.6
  61.9 3.9 %compare_select_fusion.7 = (f32[16]{0:T(128)S(1)}, f32[16]{0:T(128)S(1)}, f32[16]{0:T(128)S(1)}, f32[16]{0:T(128)S(1)}, f32[16]{0:T(128)S(1)}, /*index=5*/f32[16]{0:T(128)S(1)}) fusion(s32[24]{0:T(128)S(1)} %convert_reduce_fusion, f32[]{:T(128)} %bitcast.21, f32[]{:T(128)} %bitcast.30, f32[]{:T(128)} %bitcast.29, f32[]{:T(128)} %bitcast.28, f32[]{:T(128)} %bitcast.26, ...), kind=kLoop, calls=%fused_computation.151 | loop fusion | flops 192 | bytes 856 | tf_op jit(solution)/shard_map/mul | solution.py:69
  65.8 4.1 %fusion.83 = (f32[2048,128]{1,0:T(8,128)S(1)}, f32[2048,128]{1,0:T(8,128)S(1)}) fusion(s32[128]{0:T(128)S(1)} %iota_add_fusion), kind=kLoop, calls=%fused_computation.130 | loop fusion | flops 3932160 | bytes 2097664 | tf_op jit(solution)/shard_map/cos | solution.py:40
  70.2 95.0 %all-reduce.3.cloned.1.call-done = (bf16[8,32,2,2048]{3,1,2,0:T(8,128)(2,1)}, bf16[8,32,2,2048]{3,1,2,0:T(8,128)(2,1)}) async-done(((bf16[8,32,2,2048]{3,1,2,0:T(8,128)(2,1)}, bf16[8,32,2,2048]{3,1,2,0:T(8,128)(2,1)}), (bf16[8,32,2,2048]{3,1,2,0:T(8,128)(2,1)}, bf16[8,32,2,2048]{3,1,2,0:T(8,128)(2,1)})) %all-reduce.3.cloned.1.call-update) | async-done | bytes 4194320 | tf_op jit(solution)/shard_map/psum | solution.py:10
  165.4 29.9 %while.21 = (s32[]{:T(128)}, f32[8,32,16,128]{3,2,1,0:T(8,128)S(1)}, bf16[8,32,2,2048]{3,1,2,0:T(8,128)(2,1)}, bf16[16,2,2048]{2,0,1:T(8,128)(2,1)S(1)}, bf16[4096,128]{1,0:T(8,128)(2,1)S(1)}, /*index=5*/s32[]{:T(128)}) while((s32[]{:T(128)}, f32[8,32,16,128]{3,2,1,0:T(8,128)S(1)}, bf16[8,32,2,2048]{3,1,2,0:T(8,128)(2,1)}, ...), condition=%wide.region_5.6_spmd, body=%wide.region_4.5_spmd.sunk | while | flops 553844736 | bytes 12189773 | solution.py:108
  166.4 1.4 add_convert_fusion.5
  167.9 1.2 fusion.110
  170.2 1.4 add_convert_fusion.5
  171.6 1.2 fusion.110
  173.9 1.4 add_convert_fusion.5
  177.7 1.4 add_convert_fusion.5
  179.1 1.2 fusion.110
  181.4 1.4 add_convert_fusion.5
  185.1 1.4 add_convert_fusion.5
  188.9 1.4 add_convert_fusion.5
  190.3 1.2 fusion.110
  192.6 1.4 add_convert_fusion.5
  194.1 1.2 fusion.110
  195.3 1.3 copy-done.1
  196.8 29.9 %while.20 = (s32[]{:T(128)}, f32[8,32,16,128]{3,2,1,0:T(8,128)S(1)}, bf16[8,32,2,2048]{3,1,2,0:T(8,128)(2,1)}, bf16[16,2,2048]{2,0,1:T(8,128)(2,1)S(1)}, bf16[4096,128]{1,0:T(8,128)(2,1)S(1)}, /*index=5*/s32[]{:T(128)}) while((s32[]{:T(128)}, f32[8,32,16,128]{3,2,1,0:T(8,128)S(1)}, bf16[8,32,2,2048]{3,1,2,0:T(8,128)(2,1)}, ...), condition=%wide.region_2.3_spmd, body=%wide.region_1.2_spmd.sunk | while | flops 553844736 | bytes 12189773 | solution.py:108
  197.9 1.4 add_convert_fusion.4
  199.3 1.2 fusion.106
  201.6 1.4 add_convert_fusion.4
  205.4 1.4 add_convert_fusion.4
  206.8 1.2 fusion.106
  209.1 1.4 add_convert_fusion.4
  212.8 1.4 add_convert_fusion.4
  216.6 1.4 add_convert_fusion.4
  218.0 1.2 fusion.106
  220.3 1.4 add_convert_fusion.4
  221.8 1.2 fusion.106
  224.1 1.4 add_convert_fusion.4
  226.8 2.7 fusion.28
  229.7 4.1 %collective-permute-start = (f32[256,4,128]{2,1,0:T(4,128)S(1)}, f32[256,4,128]{2,1,0:T(4,128)S(1)}, u32[]{:S(2)}, u32[]{:S(2)}) collective-permute-start(f32[256,4,128]{2,1,0:T(4,128)S(1)} %get-tuple-element.92), channel_id=1, source_target_pairs={{0,1},{1,2},{2,3},{3,4},{4,5},{5,6},{6,7},{7,8},{8,9},{9,10},{10,1... | collective-permute-start | bytes 1572872 | tf_op jit(solution)/shard_map/ppermute | solution.py:18
  233.8 2.1 collective-permute-start.1
  236.1 3.6 %collective-permute-start.2 = (f32[256,4,128]{2,1,0:T(4,128)S(1)}, f32[256,4,128]{2,1,0:T(4,128)S(1)}, u32[]{:S(2)}, u32[]{:S(2)}) collective-permute-start(f32[256,4,128]{2,1,0:T(4,128)S(1)} %get-tuple-element.96), channel_id=1, source_target_pairs={{0,1},{1,2},{2,3},{3,4},{4,5},{5,6},{6,7},{7,8},{8,9},{9,10},{10,1... | collective-permute-start | bytes 1572872 | tf_op jit(solution)/shard_map/ppermute | solution.py:18
  239.7 1.9 collective-permute-start.3
  242.1 2.3 pad_maximum_fusion
  245.5 8.8 %collective-permute-done.1 = f32[256,4,128]{2,1,0:T(4,128)S(1)} collective-permute-done((f32[256,4,128]{2,1,0:T(4,128)S(1)}, f32[256,4,128]{2,1,0:T(4,128)S(1)}, u32[]{:S(2)}, u32[]{:S(2)}) %collective-permute-start.1) | collective-permute-done | bytes 524320 | tf_op jit(solution)/shard_map/ppermute | solution.py:21
  254.3 3.9 %fusion.55 = f32[1,256,16,128]{3,2,1,0:T(8,128)S(1)} fusion(f32[256,16,128]{2,1,0:T(8,128)S(1)} %get-tuple-element.94, f32[256,4,128]{2,1,0:T(4,128)S(1)} %collective-permute-done.1, f32[256,4,128]{2,1,0:T(4,128)S(1)} %collective-permute-done, f32[16]{0:T(128)S(1)} %get-tuple-element.122, f32[16]{0:T(128)S(1)} %get-tuple-element.107, ...), kind=kLoop, calls=%fused_computation.91 | loop fusion | flops 13107200 | bytes 5243396 | tf_op jit(solution)/shard_map/stack | solution.py:115
  258.2 1.7 collective-permute-done.3
  259.9 3.9 %fusion.34 = f32[1,256,16,128]{3,2,1,0:T(8,128)S(1)} fusion(f32[256,16,128]{2,1,0:T(8,128)S(1)} %get-tuple-element.95, f32[256,4,128]{2,1,0:T(4,128)S(1)} %collective-permute-done.3, f32[256,4,128]{2,1,0:T(4,128)S(1)} %collective-permute-done.2, f32[16]{0:T(128)S(1)} %get-tuple-element.122, f32[16]{0:T(128)S(1)} %get-tuple-element.107, ...), kind=kLoop, calls=%fused_computation.70 | loop fusion | flops 13107200 | bytes 5243396 | tf_op jit(solution)/shard_map/stack | solution.py:115
  263.8 2.3 pad_maximum_fusion.1
  (88 shorter events, 31.4 us)
Async XLA Ops:
  7.2 47.0 %all-gather.2.cloned.1.call-start = ((), (), s32[]{:S(2)}) async-start(), calls=%async_computation | async-start | bytes 2228224 | tf_op jit(solution)/shard_map/all_gather | solution.py:104
  9.2 155.9 %all-reduce.3.cloned.1.call-start = ((), (), s32[]{:S(2)}) async-start(), calls=%async_computation.1 | async-start | bytes 8388608 | tf_op jit(solution)/shard_map/psum | solution.py:10
  58.9 0.7 copy-start.5
  58.9 0.9 copy-start.4
  70.0 95.4 %copy-start = (bf16[16,2,2048]{2,0,1:T(8,128)(2,1)S(1)}, bf16[16,2,2048]{2,0,1:T(8,128)(2,1)}, u32[]{:S(2)}) copy-start(bf16[16,2,2048]{2,0,1:T(8,128)(2,1)} %pad_maximum_fusion.6) | copy-start | bytes 393220
  195.3 1.3 copy-start.1
  229.5 12.2 %copy-start.2 = (f32[8,32,16,128]{3,2,1,0:T(8,128)S(1)}, f32[8,32,16,128]{3,2,1,0:T(8,128)}, u32[]{:S(2)}) copy-start(f32[8,32,16,128]{3,2,1,0:T(8,128)} %copy-done.1) | copy-start | bytes 6291460
  229.5 12.2 %copy-start.3 = (bf16[2,256,16,128]{3,2,1,0:T(8,128)(2,1)S(1)}, bf16[2,256,16,128]{3,2,1,0:T(8,128)(2,1)}, u32[]{:S(2)}) copy-start(bf16[2,256,16,128]{3,2,1,0:T(8,128)(2,1)} %param.10) | copy-start | bytes 6291460
  229.7 15.8 %collective-permute-start = (f32[256,4,128]{2,1,0:T(4,128)S(1)}, f32[256,4,128]{2,1,0:T(4,128)S(1)}, u32[]{:S(2)}, u32[]{:S(2)}) collective-permute-start(f32[256,4,128]{2,1,0:T(4,128)S(1)} %get-tuple-element.92), channel_id=1, source_target_pairs={{0,1},{1,2},{2,3},{3,4},{4,5},{5,6},{6,7},{7,8},{8,9},{9,10},{10,1... | collective-permute-start | bytes 1572872 | tf_op jit(solution)/shard_map/ppermute | solution.py:18
  233.8 20.5 %collective-permute-start.1 = (f32[256,4,128]{2,1,0:T(4,128)S(1)}, f32[256,4,128]{2,1,0:T(4,128)S(1)}, u32[]{:S(2)}, u32[]{:S(2)}) collective-permute-start(f32[256,4,128]{2,1,0:T(4,128)S(1)} %get-tuple-element.93), channel_id=1, source_target_pairs={{1,0},{2,1},{3,2},{4,3},{5,4},{6,5},{7,6},{8,7},{9,8},{10,9},{11,1... | collective-permute-start | bytes 1572872 | tf_op jit(solution)/shard_map/ppermute | solution.py:21
  236.1 22.2 %collective-permute-start.2 = (f32[256,4,128]{2,1,0:T(4,128)S(1)}, f32[256,4,128]{2,1,0:T(4,128)S(1)}, u32[]{:S(2)}, u32[]{:S(2)}) collective-permute-start(f32[256,4,128]{2,1,0:T(4,128)S(1)} %get-tuple-element.96), channel_id=1, source_target_pairs={{0,1},{1,2},{2,3},{3,4},{4,5},{5,6},{6,7},{7,8},{8,9},{9,10},{10,1... | collective-permute-start | bytes 1572872 | tf_op jit(solution)/shard_map/ppermute | solution.py:18
  239.7 20.2 %collective-permute-start.3 = (f32[256,4,128]{2,1,0:T(4,128)S(1)}, f32[256,4,128]{2,1,0:T(4,128)S(1)}, u32[]{:S(2)}, u32[]{:S(2)}) collective-permute-start(f32[256,4,128]{2,1,0:T(4,128)S(1)} %get-tuple-element.97), channel_id=1, source_target_pairs={{1,0},{2,1},{3,2},{4,3},{5,4},{6,5},{7,6},{8,7},{9,8},{10,9},{11,1... | collective-permute-start | bytes 1572872 | tf_op jit(solution)/shard_map/ppermute | solution.py:21
Sparse Core Ops, SparseCore 0:
  10.2 43.9 all-gather.1
  59.1 106.0 all-reduce.2
where the time goes:
time: 274 us; the launch traced here: 273 us
  waiting for transfers between devices  149 us (54%)
  other arithmetic  51.5 us (19%)
  local copies, waits for them, and re-layouts  24.5 us (9%)
  matrix products  20 us (7%)
  between operations  15.6 us (6%)
  starting transfers between devices  11.8 us (4%)
    psum x1, waiting for transfers between devices, from_root(): return lax.psum(kept, axis)  95 us
    all_gather x1, waiting for transfers between devices, shards(): whole = lax.all_gather(own, 'dev', axis=0, tiled=True)  42.2 us
    another operation x18, other arithmetic  22.8 us
    dot_general x16, matrix products, cross_block(): result = jnp.dot(flat, table, preferred_element_type=jnp.float32)  20 us
    squeeze x16, local copies, waits for them, and re-layouts, shards(): corr = lax.map(lambda block: cross_block(block, own, table), grouped)  15.5 us
    ppermute x2, waiting for transfers between devices, extended_2(): lax.ppermute(lax.slice_in_dim(block, 0, width, axis=dim), axis, backward)  10.5 us
    another operation x3, other arithmetic, shards(): filtered = jnp.stack(filtered_list, axis=0)  10.1 us
    ppermute x2, starting transfers between devices, extended_2(): lax.ppermute(lax.slice_in_dim(block, block.shape[dim] - width, None, axis...  7.73 us
  transfers between devices with their start and end apart: 6, of which 5 were waited for; matrix products, arithmetic and copies ran while one was open for 7% of the time, Pallas kernels for 0%

commit v1 on v0

--- a/solution.py
+++ b/solution.py
@@ -5,9 +5,15 @@
 from jax.sharding import PartitionSpec as P
 
 
+def summed_here(x, mesh_axis):
+    parts = lax.all_gather(x, mesh_axis, axis=0, tiled=False)
+    summed = parts.sum(axis=0)
+    return summed
+
+
 def from_root(value, axis, source):
     kept = jnp.where(lax.axis_index(axis) == source, value, 0).astype(value.dtype)
-    return lax.psum(kept, axis)
+    return summed_here(kept, axis)
 
 
 def extended_2(block, sides, width):

time: 274 us -> 254 us (0.927)
  waiting for transfers between devices: 149 us -> 121 us
  other arithmetic: 51.5 us -> 63.4 us
  local copies, waits for them, and re-layouts: 24.5 us -> 21.1 us
    psum x1 -> x0, waiting for transfers between devices: 95 us -> none  [from_root(): return lax.psum(kept, axis)]
    all_gather x0 -> x2, waiting for transfers between devices: none -> 66.8 us  [summed_here(): parts = lax.all_gather(x, mesh_axis, axis=0, tiled=False)]
    reduce_sum x0 -> x2, other arithmetic: none -> 10.2 us  [summed_here(): summed = parts.sum(axis=0)]
    reshape x3 -> x1, local copies, waits for them, and re-layouts: 2.99 us -> 0.08 us  [the longest x2 2.91 us: shards(): grouped = sources.reshape(source_count // block_rows, block_rows, 2, freqs)]
  transfers between devices with their start and end apart: 6 -> 7, of which waited for: 5 -> 6; matrix products, arithmetic and copies ran while one was open for 7% -> 21% of each run, Pallas kernels for 0% -> 0%
where the time goes in v1:
time: 254 us; the launch traced here: 253 us
  waiting for transfers between devices  121 us (48%)
  other arithmetic  63.4 us (25%)
  local copies, waits for them, and re-layouts  21.1 us (8%)
  matrix products  20 us (8%)
  between operations  15.3 us (6%)
  starting transfers between devices  11.7 us (5%)
    all_gather x2, waiting for transfers between devices, summed_here(): parts = lax.all_gather(x, mesh_axis, axis=0, tiled=False)  66.8 us
    all_gather x1, waiting for transfers between devices, shards(): whole = lax.all_gather(own, 'dev', axis=0, tiled=True)  42.2 us
    another operation x18, other arithmetic  22.8 us
    dot_general x16, matrix products, cross_block(): result = jnp.dot(flat, table, preferred_element_type=jnp.float32)  20 us
    squeeze x16, local copies, waits for them, and re-layouts, shards(): corr = lax.map(lambda block: cross_block(block, own, table), grouped)  15.7 us
    ppermute x2, waiting for transfers between devices, extended_2(): lax.ppermute(lax.slice_in_dim(block, 0, width, axis=dim), axis, backward)  10.5 us
    reduce_sum x2, other arithmetic, summed_here(): summed = parts.sum(axis=0)  10.2 us
    another operation x3, other arithmetic, shards(): filtered = jnp.stack(filtered_list, axis=0)  10 us
  transfers between devices with their start and end apart: 7, of which 6 were waited for; matrix products, arithmetic and copies ran while one was open for 21% of the time, Pallas kernels for 0%

profile of v1, /device:TPU:1, one launch (start us, length us, event | category | flops | bytes accessed | tf_op | source)
XLA Modules:
  0.0 253.1 jit_solution(4805661291233275801)
XLA Ops:
  9.3 1.3 fusion.94
  12.0 42.2 %all-gather.6.cloned.1.call-done = bf16[256,2,2048]{2,0,1:T(8,128)(2,1)} async-done(((bf16[16,2,2048]{2,0,1:T(8,128)(2,1)}), bf16[256,2,2048]{2,0,1:T(8,128)(2,1)}) %all-gather.6.cloned.1.call-update) | async-done | bytes 2097168 | tf_op jit(solution)/shard_map/all_gather | solution.py:110
  54.1 3.9 %broadcast_select_fusion.1 = (bf16[256,2,2048]{2,0,1:T(8,128)(2,1)}, bf16[256,2,2048]{2,0,1:T(8,128)(2,1)}) fusion(bf16[256,2,2048]{2,0,1:T(8,128)(2,1)} %all-gather.6.cloned.1.call-done, pred[]{:T(512)S(6)} %eq.36, pred[]{:T(512)S(6)} %eq.37), kind=kLoop, calls=%fused_computation.119 | loop fusion | flops 2097152 | bytes 6291458 | tf_op jit(solution)/shard_map/jit(_where)/select_n | solution.py:15
  59.7 1.3 compare_select_fusion.6
  61.0 3.8 %compare_select_fusion.7 = (f32[16]{0:T(128)S(1)}, f32[16]{0:T(128)S(1)}, f32[16]{0:T(128)S(1)}, f32[16]{0:T(128)S(1)}, f32[16]{0:T(128)S(1)}, /*index=5*/f32[16]{0:T(128)S(1)}) fusion(s32[24]{0:T(128)S(1)} %convert_reduce_fusion, f32[]{:T(128)} %bitcast.23, f32[]{:T(128)} %bitcast.32, f32[]{:T(128)} %bitcast.31, f32[]{:T(128)} %bitcast.30, f32[]{:T(128)} %bitcast.28, ...), kind=kLoop, calls=%fused_computation.151 | loop fusion | flops 192 | bytes 856 | tf_op jit(solution)/shard_map/mul | solution.py:75
  64.8 4.1 %fusion.83 = (f32[2048,128]{1,0:T(8,128)S(1)}, f32[2048,128]{1,0:T(8,128)S(1)}) fusion(s32[128]{0:T(128)S(1)} %iota_add_fusion), kind=kLoop, calls=%fused_computation.130 | loop fusion | flops 3932160 | bytes 2097664 | tf_op jit(solution)/shard_map/cos | solution.py:46
  69.1 44.0 %all-gather.10.cloned.1.call-done = bf16[512,2,2048]{2,0,1:T(8,128)(2,1)} async-done(((bf16[256,2,2048]{2,0,1:T(8,128)(2,1)}), bf16[512,2,2048]{2,0,1:T(8,128)(2,1)}) %all-gather.10.cloned.1.call-update) | async-done | bytes 4194320 | tf_op jit(solution)/shard_map/all_gather | solution.py:9
  113.1 5.1 %reduce_sum.34 = bf16[256,2,2048]{2,0,1:T(8,128)(2,1)} reduce(bf16[2,256,2,2048]{3,1,0,2:T(8,128)(2,1)} %bitcast.115, bf16[]{:T(256)} %constant.100.clone.1), dimensions={0}, to_apply=%region_3.4 | reduce | flops 1048576 | bytes 6291458 | tf_op jit(solution)/shard_map/reduce_sum | solution.py:10
  119.1 30.0 %while.21 = (s32[]{:T(128)}, f32[8,32,16,128]{3,2,1,0:T(8,128)S(1)}, bf16[8,32,2,2048]{3,1,0,2:T(8,128)(2,1)}, bf16[16,2,2048]{2,0,1:T(8,128)(2,1)S(1)}, bf16[4096,128]{1,0:T(8,128)(2,1)S(1)}, /*index=5*/s32[]{:T(128)}) while((s32[]{:T(128)}, f32[8,32,16,128]{3,2,1,0:T(8,128)S(1)}, bf16[8,32,2,2048]{3,1,0,2:T(8,128)(2,1)}, ...), condition=%wide.region_5.6_spmd, body=%wide.region_4.5_spmd.sunk | while | flops 553844736 | bytes 12189773 | solution.py:114
  120.1 1.4 add_convert_fusion.5
  121.5 1.2 fusion.110
  123.9 1.4 add_convert_fusion.5
  125.3 1.2 fusion.110
  127.7 1.4 add_convert_fusion.5
  129.1 1.2 fusion.110
  131.4 1.4 add_convert_fusion.5
  135.2 1.4 add_convert_fusion.5
  136.6 1.2 fusion.110
  138.9 1.4 add_convert_fusion.5
  142.7 1.4 add_convert_fusion.5
  144.1 1.2 fusion.110
  146.4 1.4 add_convert_fusion.5
  147.8 1.2 fusion.110
  149.1 22.9 %all-gather.8.cloned.1.call-done = bf16[512,2,2048]{2,0,1:T(8,128)(2,1)} async-done(((bf16[256,2,2048]{2,0,1:T(8,128)(2,1)}), bf16[512,2,2048]{2,0,1:T(8,128)(2,1)}) %all-gather.8.cloned.1.call-update) | async-done | bytes 4194320 | tf_op jit(solution)/shard_map/all_gather | solution.py:9
  172.0 5.1 %reduce_sum.33 = bf16[256,2,2048]{2,0,1:T(8,128)(2,1)} reduce(bf16[2,256,2,2048]{3,1,0,2:T(8,128)(2,1)} %bitcast.116, bf16[]{:T(256)} %constant.100.clone.1), dimensions={0}, to_apply=%region_0.1 | reduce | flops 1048576 | bytes 6291458 | tf_op jit(solution)/shard_map/reduce_sum | solution.py:10
  177.2 30.0 %while.20 = (s32[]{:T(128)}, f32[8,32,16,128]{3,2,1,0:T(8,128)S(1)}, bf16[8,32,2,2048]{3,1,0,2:T(8,128)(2,1)}, bf16[16,2,2048]{2,0,1:T(8,128)(2,1)S(1)}, bf16[4096,128]{1,0:T(8,128)(2,1)S(1)}, /*index=5*/s32[]{:T(128)}) while((s32[]{:T(128)}, f32[8,32,16,128]{3,2,1,0:T(8,128)S(1)}, bf16[8,32,2,2048]{3,1,0,2:T(8,128)(2,1)}, ...), condition=%wide.region_2.3_spmd, body=%wide.region_1.2_spmd.sunk | while | flops 553844736 | bytes 12189773 | solution.py:114
  178.3 1.4 add_convert_fusion.4
  182.0 1.4 add_convert_fusion.4
  183.5 1.2 fusion.106
  185.8 1.4 add_convert_fusion.4
  187.2 1.2 fusion.106
  189.5 1.4 add_convert_fusion.4
  191.0 1.2 fusion.106
  193.3 1.4 add_convert_fusion.4
  197.0 1.4 add_convert_fusion.4
  200.8 1.4 add_convert_fusion.4
  204.5 1.4 add_convert_fusion.4
  207.2 2.7 %fusion.28 = (f32[256,16,128]{2,1,0:T(8,128)S(1)}, f32[256,16,128]{2,1,0:T(8,128)S(1)}) fusion(f32[8,32,16,128]{3,2,1,0:T(8,128)S(1)} %get-tuple-element.56, bf16[2,256,16,128]{3,2,1,0:T(8,128)(2,1)} %param.10, f32[8,32,16,128]{3,2,1,0:T(8,128)} %copy-done.1), kind=kLoop, calls=%fused_computation.64 | loop fusion | flops 2097152 | bytes 10485760 | tf_op jit(solution)/shard_map/add | solution.py:116
  210.1 4.1 %collective-permute-start = (f32[256,4,128]{2,1,0:T(4,128)S(1)}, f32[256,4,128]{2,1,0:T(4,128)S(1)}, u32[]{:S(2)}, u32[]{:S(2)}) collective-permute-start(f32[256,4,128]{2,1,0:T(4,128)S(1)} %get-tuple-element.110), channel_id=1, source_target_pairs={{0,1},{1,2},{2,3},{3,4},{4,5},{5,6},{6,7},{7,8},{8,9},{9,10},{10,1... | collective-permute-start | bytes 1572872 | tf_op jit(solution)/shard_map/ppermute | solution.py:24
  214.2 1.9 collective-permute-start.1
  216.3 3.6 %collective-permute-start.2 = (f32[256,4,128]{2,1,0:T(4,128)S(1)}, f32[256,4,128]{2,1,0:T(4,128)S(1)}, u32[]{:S(2)}, u32[]{:S(2)}) collective-permute-start(f32[256,4,128]{2,1,0:T(4,128)S(1)} %get-tuple-element.114), channel_id=1, source_target_pairs={{0,1},{1,2},{2,3},{3,4},{4,5},{5,6},{6,7},{7,8},{8,9},{9,10},{10,1... | collective-permute-start | bytes 1572872 | tf_op jit(solution)/shard_map/ppermute | solution.py:24
  220.0 1.9 collective-permute-start.3
  222.4 2.3 pad_maximum_fusion
  225.9 8.8 %collective-permute-done.1 = f32[256,4,128]{2,1,0:T(4,128)S(1)} collective-permute-done((f32[256,4,128]{2,1,0:T(4,128)S(1)}, f32[256,4,128]{2,1,0:T(4,128)S(1)}, u32[]{:S(2)}, u32[]{:S(2)}) %collective-permute-start.1) | collective-permute-done | bytes 524320 | tf_op jit(solution)/shard_map/ppermute | solution.py:27
  234.7 3.9 %fusion.55 = f32[1,256,16,128]{3,2,1,0:T(8,128)S(1)} fusion(f32[256,16,128]{2,1,0:T(8,128)S(1)} %get-tuple-element.112, f32[256,4,128]{2,1,0:T(4,128)S(1)} %collective-permute-done.1, f32[256,4,128]{2,1,0:T(4,128)S(1)} %collective-permute-done, f32[16]{0:T(128)S(1)} %get-tuple-element.140, f32[16]{0:T(128)S(1)} %get-tuple-element.125, ...), kind=kLoop, calls=%fused_computation.91 | loop fusion | flops 13107200 | bytes 5243396 | tf_op jit(solution)/shard_map/stack | solution.py:121
  238.6 1.7 collective-permute-done.3
  240.4 3.9 %fusion.34 = f32[1,256,16,128]{3,2,1,0:T(8,128)S(1)} fusion(f32[256,16,128]{2,1,0:T(8,128)S(1)} %get-tuple-element.113, f32[256,4,128]{2,1,0:T(4,128)S(1)} %collective-permute-done.3, f32[256,4,128]{2,1,0:T(4,128)S(1)} %collective-permute-done.2, f32[16]{0:T(128)S(1)} %get-tuple-element.140, f32[16]{0:T(128)S(1)} %get-tuple-element.125, ...), kind=kLoop, calls=%fused_computation.70 | loop fusion | flops 13107200 | bytes 5243396 | tf_op jit(solution)/shard_map/stack | solution.py:121
  244.2 2.3 pad_maximum_fusion.1
  (91 shorter events, 32.4 us)
Async XLA Ops:
  7.2 47.0 %all-gather.6.cloned.1.call-start = ((), (), s32[]{:S(2)}) async-start(), calls=%async_computation | async-start | bytes 2228224 | tf_op jit(solution)/shard_map/all_gather | solution.py:110
  9.2 103.8 %all-gather.10.cloned.1.call-start = ((), (), s32[]{:S(2)}) async-start(), calls=%async_computation.2 | async-start | bytes 6291456 | tf_op jit(solution)/shard_map/all_gather | solution.py:9
  58.0 0.7 copy-start.5
  58.0 0.9 copy-start.4
  58.0 113.9 %all-gather.8.cloned.1.call-start = ((), (), s32[]{:S(2)}) async-start(), calls=%async_computation.1 | async-start | bytes 6291456 | tf_op jit(solution)/shard_map/all_gather | solution.py:9
  118.2 0.9 copy-start
  149.1 28.0 %copy-start.1 = (f32[8,32,16,128]{3,2,1,0:T(8,128)}, f32[8,32,16,128]{3,2,1,0:T(8,128)S(1)}, u32[]{:S(2)}) copy-start(f32[8,32,16,128]{3,2,1,0:T(8,128)S(1)} %get-tuple-element.57) | copy-start | bytes 6291460
  209.9 12.0 %copy-start.2 = (f32[8,32,16,128]{3,2,1,0:T(8,128)S(1)}, f32[8,32,16,128]{3,2,1,0:T(8,128)}, u32[]{:S(2)}) copy-start(f32[8,32,16,128]{3,2,1,0:T(8,128)} %copy-done.1) | copy-start | bytes 6291460
  209.9 12.0 %copy-start.3 = (bf16[2,256,16,128]{3,2,1,0:T(8,128)(2,1)S(1)}, bf16[2,256,16,128]{3,2,1,0:T(8,128)(2,1)}, u32[]{:S(2)}) copy-start(bf16[2,256,16,128]{3,2,1,0:T(8,128)(2,1)} %param.10) | copy-start | bytes 6291460
  210.1 15.8 %collective-permute-start = (f32[256,4,128]{2,1,0:T(4,128)S(1)}, f32[256,4,128]{2,1,0:T(4,128)S(1)}, u32[]{:S(2)}, u32[]{:S(2)}) collective-permute-start(f32[256,4,128]{2,1,0:T(4,128)S(1)} %get-tuple-element.110), channel_id=1, source_target_pairs={{0,1},{1,2},{2,3},{3,4},{4,5},{5,6},{6,7},{7,8},{8,9},{9,10},{10,1... | collective-permute-start | bytes 1572872 | tf_op jit(solution)/shard_map/ppermute | solution.py:24
  214.2 20.5 %collective-permute-start.1 = (f32[256,4,128]{2,1,0:T(4,128)S(1)}, f32[256,4,128]{2,1,0:T(4,128)S(1)}, u32[]{:S(2)}, u32[]{:S(2)}) collective-permute-start(f32[256,4,128]{2,1,0:T(4,128)S(1)} %get-tuple-element.111), channel_id=1, source_target_pairs={{1,0},{2,1},{3,2},{4,3},{5,4},{6,5},{7,6},{8,7},{9,8},{10,9},{11,1... | collective-permute-start | bytes 1572872 | tf_op jit(solution)/shard_map/ppermute | solution.py:27
  216.3 22.3 %collective-permute-start.2 = (f32[256,4,128]{2,1,0:T(4,128)S(1)}, f32[256,4,128]{2,1,0:T(4,128)S(1)}, u32[]{:S(2)}, u32[]{:S(2)}) collective-permute-start(f32[256,4,128]{2,1,0:T(4,128)S(1)} %get-tuple-element.114), channel_id=1, source_target_pairs={{0,1},{1,2},{2,3},{3,4},{4,5},{5,6},{6,7},{7,8},{8,9},{9,10},{10,1... | collective-permute-start | bytes 1572872 | tf_op jit(solution)/shard_map/ppermute | solution.py:24
  220.0 20.4 %collective-permute-start.3 = (f32[256,4,128]{2,1,0:T(4,128)S(1)}, f32[256,4,128]{2,1,0:T(4,128)S(1)}, u32[]{:S(2)}, u32[]{:S(2)}) collective-permute-start(f32[256,4,128]{2,1,0:T(4,128)S(1)} %get-tuple-element.115), channel_id=1, source_target_pairs={{1,0},{2,1},{3,2},{4,3},{5,4},{6,5},{7,6},{8,7},{9,8},{10,9},{11,1... | collective-permute-start | bytes 1572872 | tf_op jit(solution)/shard_map/ppermute | solution.py:27
Sparse Core Ops, SparseCore 0:
  10.2 43.9 all-gather.5
  58.1 54.8 all-gather.9
  115.2 56.7 all-gather.7
